TPU v7x, 512 devices: a whole 4x4x16 slice. The times are simulated.
512 devices in a mesh: row: 16 (over y, x), adp: 32 (over z, core).
Axes of the slice: x: 4, y: 4, z: 16, core: 2. Of those that a mesh axis runs over, the one named last changes fastest.
Arguments:
- tokens: bfloat16 [8192, 8192], P('row', 'adp'), may hold values from -6 to 6
- query_base_weight: bfloat16 [8192, 8192], P(None, 'adp'), may hold values from -0.0625 to 0.0625
- adapter_down_weight: bfloat16 [32, 16, 8192], P('adp'), may hold values from -0.0625 to 0.0625
- adapter_up_weight: bfloat16 [32, 16, 8192], P('adp'), may hold values from -1.5 to 1.5
- row_adapter_index: int32 [8192, 1], P('row'), may hold values from 0 to 31; in each aligned block of 512 rows (0 to 511, 512 to 1023, ...) at most 64 rows name the same one
Outputs:
- queries: bfloat16 [8192, 8192], P('row', 'adp')
Inputs may be any that keep to these rules, and one draw needn't show every extreme that they name: `row_adapter_index`: among the 512 rows of one index of row, no adapter is used by more than 64 rows, and some adapter is used by exactly 64 rows; every adapter is used by some row.
All inputs are finite; a program needn't handle non-finite values.
Results may differ from a plain program's by a relative error of at most 0.0055.
Values may be sent and summed in bfloat16 or wider, within the bound.
No kernel may reach another device: no remote copies, remote signals or barrier semaphores. Data moves between devices by JAX's collectives and lax.ppermute only.
A program may use at most 64 MiB of HBM per device.

v0:
```python
import jax
import jax.numpy as jnp
from jax import lax
from jax.sharding import PartitionSpec as P

ADAPTER_RANK = 16
SCALE_NUMERATOR = 32


def shards(tokens, query_base_weight, adapter_down_weight, adapter_up_weight, row_adapter_index):
    row_count = tokens.shape[0]
    total_width = query_base_weight.shape[0]
    local_row_count = adapter_down_weight.shape[0]
    rank_length = adapter_down_weight.shape[1]
    groups = lax.axis_size("adp")
    total_adapters = local_row_count * groups
    capacity = 4 * row_count // total_adapters
    position = lax.axis_index("adp")
    adapter_scale = SCALE_NUMERATOR / ADAPTER_RANK
    down_weight_flat = adapter_down_weight.reshape(local_row_count * rank_length, total_width)
    shard_piece = lax.all_gather(tokens, "adp", axis=1, tiled=True)
    base_part = jnp.dot(shard_piece, query_base_weight, preferred_element_type=jnp.float32)
    down_part = lax.dot_general(
        shard_piece, down_weight_flat, (((1,), (1,)), ((), ())), preferred_element_type=jnp.float32
    )
    adapter_of = row_adapter_index[:, 0]
    every_match = adapter_of[:, None] == jnp.arange(total_adapters, dtype=jnp.int32)[None, :]
    owned_match = lax.dynamic_slice_in_dim(
        every_match, position * local_row_count, local_row_count, 1
    )
    rank_own = jnp.where(
        jnp.repeat(owned_match, rank_length, axis=1), down_part, jnp.zeros_like(down_part)
    ).astype(jnp.bfloat16)
    order_in = jnp.cumsum(every_match.astype(jnp.int32), axis=0) - 1
    slot_index = jnp.arange(capacity, dtype=jnp.int32)
    slot_table = (
        every_match.T[:, None, :] & (order_in.T[:, None, :] == slot_index[None, :, None])
    ).astype(jnp.bfloat16)
    own_table = lax.dynamic_slice_in_dim(slot_table, position * local_row_count, local_row_count, 0)
    selected_rows = jnp.einsum(
        "acn,nak->ack",
        own_table,
        rank_own.reshape(row_count, local_row_count, rank_length),
        preferred_element_type=jnp.float32,
    ).astype(jnp.bfloat16)
    update_rows = (
        jnp.einsum(
            "vbf,vfx->vbx", selected_rows, adapter_up_weight, preferred_element_type=jnp.float32
        )
        * adapter_scale
    ).astype(jnp.bfloat16)
    arrived = lax.all_to_all(
        update_rows.reshape(local_row_count * capacity, total_width),
        "adp",
        split_axis=1,
        concat_axis=0,
        tiled=True,
    )
    update = lax.dot_general(
        slot_table.reshape(total_adapters * capacity, row_count),
        arrived,
        (((0,), (0,)), ((), ())),
        preferred_element_type=jnp.float32,
    ).astype(jnp.bfloat16)
    update = lax.optimization_barrier(update)
    return (base_part + update.astype(jnp.float32)).astype(jnp.bfloat16)


def solution(mesh):
    return jax.shard_map(
        shards,
        mesh=mesh,
        in_specs=(
            P("row", "adp"),
            P(None, "adp"),
            P("adp", None, None),
            P("adp", None, None),
            P("row", None),
        ),
        out_specs=P("row", "adp"),
        check_vma=False,
    )
```

profile of v0, /device:TPU:1, one launch (start us, length us, event | category | flops | bytes accessed | tf_op | source)
XLA Modules:
  0.0 193.7 jit_solution(11247434372727005446)
XLA Ops:
  6.5 0.0 copy-start
  6.5 0.0 all-gather.2.cloned.1.call-start
  6.5 0.7 all-gather.2.cloned.1.call-update
  7.3 0.7 fusion.15
  8.0 1.2 reduce-window.6
  9.1 0.2 slice_reduce_fusion
  9.4 0.7 compare_reduce_fusion
  10.1 0.7 iota_compare_fusion.2
  10.8 0.1 copy_bitcast_fusion.1
  10.9 0.9 fusion.1
  11.8 98.9 %all-gather.2.cloned.1.call-done = bf16[512,8192]{1,0:T(8,128)(2,1)} async-done(((bf16[512,256]{1,0:T(8,128)(2,1)}), bf16[512,8192]{1,0:T(8,128)(2,1)}) %all-gather.2.cloned.1.call-update) | async-done | bytes 8388624 | tf_op jit(solution)/shard_map/all_gather | solution.py:21
  110.7 5.8 %fusion.6 = bf16[64,16]{1,0:T(8,128)(2,1)S(1)} fusion(bf16[512,8192]{1,0:T(8,128)(2,1)} %all-gather.2.cloned.1.call-done, bf16[1,16,8192]{2,1,0:T(8,128)(2,1)} %param.7, pred[512]{0:T(512)(128)(4,1)S(1)} %compare_reduce_fusion, pred[32,64,512]{2,1,0:T(32,128)(4,1)S(1)} %fusion.1, s32[]{:T(128)S(6)} %select_n.8), kind=kOutput, calls=%fused_computation.11 | convolution fusion | flops 135283712 | bytes 8686084 | tf_op jit(solution)/shard_map/acn,nak->ack/dot_general | solution.py:40
  116.5 0.0 copy-done
  116.5 0.4 fusion
  117.0 0.0 slice-start
  117.0 0.1 copy.13
  117.1 63.3 %all_to_all.16 = bf16[64,32,256]{2,0,1:T(8,128)(2,1)S(1)} all-to-all(bf16[64,32,256]{2,0,1:T(8,128)(2,1)S(1)} %bitcast.33), channel_id=1, replica_groups=mesh['row'=16,'adp'=32] {'adp'}, dimensions={1} | all-to-all | bytes 2097152 | tf_op jit(solution)/shard_map/all_to_all | solution.py:52
  180.4 0.0 slice-start.1
  180.4 0.0 copy-start.1
  180.4 1.3 fusion.3
  181.7 0.0 slice-done
  181.7 0.9 slice-done.1
  182.6 1.3 copy-done.1
  183.8 3.0 %fusion.2 = bf16[512,256]{1,0:T(8,128)(2,1)} fusion(bf16[512,8192]{1,0:T(8,128)(2,1)S(1)} %bitcast.38, bf16[8192,256]{1,0:T(8,128)(2,1)S(1)} %copy-done.1, bf16[512,256]{1,0:T(8,128)(2,1)S(1)} %fusion.3), kind=kOutput, calls=%fused_computation.6 | convolution fusion | flops 2147876864 | bytes 13107200 | tf_op jit(solution)/shard_map/dot_general | solution.py:22
  (3 shorter events, 0.0 us)
Async XLA Ops:
  6.5 110.0 %copy-start = (bf16[1,16,8192]{2,1,0:T(8,128)(2,1)S(1)}, bf16[1,16,8192]{2,1,0:T(8,128)(2,1)}, u32[]{:S(2)}) copy-start(bf16[1,16,8192]{2,1,0:T(8,128)(2,1)} %param.8) | copy-start | bytes 786436
  6.5 104.2 %all-gather.2.cloned.1.call-start = ((), (), s32[]{:S(2)}) async-start(), calls=%async_computation.1 | async-start | bytes 8650752 | tf_op jit(solution)/shard_map/all_gather | solution.py:21
  117.0 64.7 %slice-start = ((s8[8388608]{0:T(1024)(128)(4,1)}), s8[4194304]{0:T(1024)(128)(4,1)S(1)}, s32[]{:S(2)}) async-start(s8[8388608]{0:T(1024)(128)(4,1)} %bitcast.37), calls=%async_computation.2 | async-start | bytes 8388608
  180.4 2.2 %slice-start.1 = ((s8[8388608]{0:T(1024)(128)(4,1)}), s8[4194304]{0:T(1024)(128)(4,1)S(1)}, s32[]{:S(2)}) async-start(s8[8388608]{0:T(1024)(128)(4,1)} %bitcast.37), calls=%async_computation.3 | async-start | bytes 8388608
  180.4 3.5 %copy-start.1 = (bf16[8192,256]{1,0:T(8,128)(2,1)S(1)}, bf16[8192,256]{1,0:T(8,128)(2,1)}, u32[]{:S(2)}) copy-start(bf16[8192,256]{1,0:T(8,128)(2,1)} %param.6) | copy-start | bytes 12582916
Sparse Core Ops, SparseCore 0:
  9.4 101.2 all-gather.1
where the time goes:
time: 194 us
  waiting for transfers between devices  99.6 us (51%)
  blocking collectives  63.3 us (33%)
  between operations  13.5 us (7%)
  matrix products  10.6 us (5%)
  other arithmetic  4.29 us (2%)
  local copies, waits for them, and re-layouts  2.49 us (1%)
    all_gather x1, waiting for transfers between devices, shards(): shard_piece = lax.all_gather(tokens, 'adp', axis=1, tiled=True)  98.9 us
    all_to_all x1, blocking collectives, shards(): lax.all_to_all(update_rows.reshape(local_row_count * capacity, total_widt...  63.3 us
    dot_general x1, matrix products, shards(): jnp.einsum('acn,nak->ack', own_table, rank_own.reshape(row_count, local_r...  5.83 us
  transfers between devices with their start and end apart: 1, of which 1 were waited for; matrix products, arithmetic and copies ran while one was open for 2% of the time, Pallas kernels for 0%

commit v1 on v0

--- a/solution.py
+++ b/solution.py
@@ -18,7 +18,9 @@
     position = lax.axis_index("adp")
     adapter_scale = SCALE_NUMERATOR / ADAPTER_RANK
     down_weight_flat = adapter_down_weight.reshape(local_row_count * rank_length, total_width)
-    shard_piece = lax.all_gather(tokens, "adp", axis=1, tiled=True)
+    shaped = jnp.stack([tokens for _ in range(lax.axis_size("adp"))])
+    field_out = lax.all_to_all(shaped, "adp", 0, 0)
+    shard_piece = jnp.concatenate(field_out, axis=1)
     base_part = jnp.dot(shard_piece, query_base_weight, preferred_element_type=jnp.float32)
     down_part = lax.dot_general(
         shard_piece, down_weight_flat, (((1,), (1,)), ((), ())), preferred_element_type=jnp.float32

time: 194 us -> 466 us (2.40)
  waiting for transfers between devices: 99.6 us -> 358 us
  starting transfers between devices: 0.01 us -> 16.9 us
  between operations: 13.5 us -> 0.1 us
  blocking collectives: 63.3 us -> 68.3 us
    all_to_all x0 -> x1, waiting for transfers between devices: none -> 358 us  [shards(): field_out = lax.all_to_all(shaped, 'adp', 0, 0)]
    all_gather x1 -> x0, waiting for transfers between devices: 98.9 us -> none  [shards(): shard_piece = lax.all_gather(tokens, 'adp', axis=1, tiled=True)]
    all_to_all x0 -> x1, starting transfers between devices: none -> 16.9 us  [shards(): field_out = lax.all_to_all(shaped, 'adp', 0, 0)]
    all_to_all x1, blocking collectives: 63.3 us -> 68.3 us  [shards(): lax.all_to_all(update_rows.reshape(local_row_count * capacity, total_widt...]
  transfers between devices with their start and end apart: 1 -> 1, of which waited for: 1 -> 1; matrix products, arithmetic and copies ran while one was open for 2% -> 1% of each run, Pallas kernels for 0% -> 0%
where the time goes in v1:
time: 466 us
  waiting for transfers between devices  358 us (77%)
  blocking collectives  68.3 us (15%)
  starting transfers between devices  16.9 us (4%)
  matrix products  14.1 us (3%)
  local copies, waits for them, and re-layouts  6.51 us (1%)
    all_to_all x1, waiting for transfers between devices, shards(): field_out = lax.all_to_all(shaped, 'adp', 0, 0)  358 us
    all_to_all x1, blocking collectives, shards(): lax.all_to_all(update_rows.reshape(local_row_count * capacity, total_widt...  68.3 us
    all_to_all x1, starting transfers between devices, shards(): field_out = lax.all_to_all(shaped, 'adp', 0, 0)  16.9 us
  transfers between devices with their start and end apart: 1, of which 1 were waited for; matrix products, arithmetic and copies ran while one was open for 1% of the time, Pallas kernels for 0%

profile of v1, /device:TPU:1, one launch (start us, length us, event | category | flops | bytes accessed | tf_op | source)
XLA Modules:
  0.0 466.2 jit_solution(11368300762481408209)
XLA Ops:
  0.0 0.0 copy-start
  0.0 1.1 copy.7
  1.1 4.2 stack.2
  5.3 0.0 copy-start.2
  5.3 0.0 copy-start.3
  5.3 16.9 %all-to-all-start = ((bf16[32,512,256]{1,2,0:T(8,128)(2,1)}), bf16[32,512,256]{1,2,0:T(8,128)(2,1)}, u32[]{:S(2)}, u32[]{:S(2)}) async-start(bf16[32,512,256]{1,2,0:T(8,128)(2,1)} %stack.2), calls=%async_computation | async-start | bytes 16777216 | tf_op jit(solution)/shard_map/all_to_all | solution.py:22
  22.2 0.0 copy-done.2
  22.3 1.2 reduce-window.6
  23.4 0.2 slice_reduce_fusion
  23.7 0.1 copy_bitcast_fusion.1
  23.8 0.9 fusion.1
  24.8 358.1 %all-to-all-done = bf16[32,512,256]{1,2,0:T(8,128)(2,1)} async-done(((bf16[32,512,256]{1,2,0:T(8,128)(2,1)}), bf16[32,512,256]{1,2,0:T(8,128)(2,1)}, u32[]{:S(2)}, u32[]{:S(2)}) %all-to-all-start) | async-done | bytes 8388640 | tf_op jit(solution)/shard_map/all_to_all | solution.py:22
  382.8 0.0 copy-done.3
  382.8 5.9 %fusion.6 = bf16[64,16]{1,0:T(8,128)(2,1)S(1)} fusion(bf16[512,8192]{0,1:T(8,128)(2,1)} %bitcast.1, bf16[1,16,8192]{2,1,0:T(8,128)(2,1)S(1)} %copy-done.3, pred[512]{0:T(512)(128)(4,1)S(1)} %compare_reduce_fusion, pred[32,64,512]{2,1,0:T(32,128)(4,1)S(1)} %fusion.1, s32[]{:T(128)S(6)} %select_n.8), kind=kOutput, calls=%fused_computation.11 | convolution fusion | flops 135283712 | bytes 8686084 | tf_op jit(solution)/shard_map/acn,nak->ack/dot_general | solution.py:42
  388.7 0.0 copy-done
  388.7 0.4 fusion
  389.1 0.1 copy.14
  389.2 68.3 %all_to_all.21 = bf16[64,32,256]{2,0,1:T(8,128)(2,1)S(1)} all-to-all(bf16[64,32,256]{2,0,1:T(8,128)(2,1)S(1)} %bitcast.36), channel_id=1, replica_groups=mesh['row'=16,'adp'=32] {'adp'}, dimensions={1} | all-to-all | bytes 2097152 | tf_op jit(solution)/shard_map/all_to_all | solution.py:54
  457.5 0.0 copy-start.1
  457.5 1.3 fusion.2
  458.8 0.9 copy-done.1
  459.7 6.5 %fusion.3 = bf16[512,256]{1,0:T(8,128)(2,1)} fusion(bf16[512,8192]{0,1:T(8,128)(2,1)} %bitcast.1, bf16[8192,256]{1,0:T(8,128)(2,1)S(1)} %copy-done.1, bf16[512,256]{1,0:T(8,128)(2,1)S(1)} %fusion.2), kind=kOutput, calls=%fused_computation.7 | convolution fusion | flops 2147876864 | bytes 13107200 | tf_op jit(solution)/shard_map/dot_general | solution.py:24
  (5 shorter events, 0.1 us)
Async XLA Ops:
  0.0 388.7 %copy-start = (bf16[1,16,8192]{2,1,0:T(8,128)(2,1)S(1)}, bf16[1,16,8192]{2,1,0:T(8,128)(2,1)}, u32[]{:S(2)}) copy-start(bf16[1,16,8192]{2,1,0:T(8,128)(2,1)} %param.8) | copy-start | bytes 786436
  5.3 16.9 %copy-start.2 = (s32[512,1]{0,1:T(1,128)S(1)}, s32[512,1]{0,1:T(1,128)}, u32[]{:S(2)}) copy-start(s32[512,1]{0,1:T(1,128)} %param.9) | copy-start | bytes 6148
  5.3 377.5 %copy-start.3 = (bf16[1,16,8192]{2,1,0:T(8,128)(2,1)S(1)}, bf16[1,16,8192]{2,1,0:T(8,128)(2,1)}, u32[]{:S(2)}) copy-start(bf16[1,16,8192]{2,1,0:T(8,128)(2,1)} %param.7) | copy-start | bytes 786436
  5.3 377.5 %all-to-all-start = ((bf16[32,512,256]{1,2,0:T(8,128)(2,1)}), bf16[32,512,256]{1,2,0:T(8,128)(2,1)}, u32[]{:S(2)}, u32[]{:S(2)}) async-start(bf16[32,512,256]{1,2,0:T(8,128)(2,1)} %stack.2), calls=%async_computation | async-start | bytes 16777216 | tf_op jit(solution)/shard_map/all_to_all | solution.py:22
  457.5 2.2 copy-start.1
